TPU v7x, 128 devices: a whole 4x4x4 slice. The times are simulated.
128 devices in a mesh: row: 8 (over z, y_lo), pair: 16 (over x, y_hi, core).
Axes of the slice: x: 4, y: 4 (y_hi: 2, y_lo: 2; y = y_hi * 2 + y_lo), z: 4, core: 2. Of those that a mesh axis runs over, the one named last changes fastest.
Arguments:
- snapshots: float32 [32768, 2048], P(('row', 'pair')), may hold values from -640 to 640
- start_order: int32 [32], replicated, may hold values from 0 to 31, each once
Outputs:
- rotated: float32 [32768, 2048], P('row', 'pair')
Inputs may be any that keep to these rules, and one draw needn't show every extreme that they name: `start_order`: each of the 32 block numbers appears once.
All inputs are finite; a program needn't handle non-finite values.
Results may differ from a plain program's by a relative error of at most 0.0003.
Values sent between devices are 32-bit elements; how exact they have to be, the bound alone decides.
A program may use at most 64 MiB of HBM per device.

v0:
```python
import math

import jax
import jax.numpy as jnp
from jax import lax
from jax.sharding import PartitionSpec as P

STEPS = 12
ROOT_STEPS = 3


def from_behind(block, axis, distance):
    devices = range(lax.axis_size(axis))
    route = [(i - distance, i) for i in devices if i - distance in devices]
    return lax.ppermute(block, axis, route)


def matmul_high(left, right):
    return jnp.matmul(left, right, precision=lax.Precision.HIGHEST)


def rotation(norms, cross):
    half_width = cross.shape[-1]
    inverse_norm = lax.rsqrt(norms + 1e-06)
    cross_block = (
        cross * inverse_norm[..., :half_width, None] * inverse_norm[..., None, half_width:]
    )
    frobenius = jnp.sqrt(jnp.sum(cross_block * cross_block, axis=(-2, -1), keepdims=True))
    coupling = cross_block / (1.0 + frobenius)
    zero_block = jnp.zeros_like(coupling)
    upper = jnp.concatenate([zero_block, coupling], axis=-1)
    lower = jnp.concatenate([-jnp.swapaxes(coupling, -1, -2), zero_block], axis=-1)
    skew_matrix = jnp.concatenate([upper, lower], axis=-2)
    full_shape = skew_matrix.shape
    identity = jnp.eye(2 * half_width, dtype=cross.dtype)
    current = (identity - matmul_high(skew_matrix, skew_matrix)) * 0.5
    inverse_root = identity
    for root_number in range(ROOT_STEPS):
        correction = 1.5 * identity - 0.5 * matmul_high(inverse_root, current)
        current = matmul_high(current, correction)
        inverse_root = matmul_high(correction, inverse_root)
    return matmul_high(identity + skew_matrix, inverse_root) * (1.0 / math.sqrt(2.0))


def per_device(snapshots, start_order):
    row_count = snapshots.shape[0]
    block_count = start_order.shape[0]
    block_width = snapshots.shape[1] // block_count
    arranged = jnp.take(snapshots.reshape(row_count, block_count, block_width), start_order, axis=1)
    relaid = lax.all_to_all(
        arranged.reshape(row_count, block_count * block_width),
        "pair",
        split_axis=1,
        concat_axis=0,
        tiled=True,
    )
    position = lax.axis_index("pair")
    pair_count = lax.axis_size("pair")

    def tournament_step(step_number, pair_block):
        cross = jnp.dot(
            pair_block[:, :block_width].T,
            pair_block[:, block_width:],
            precision=lax.Precision.HIGHEST,
            preferred_element_type=jnp.float32,
        )
        norms = jnp.sum(pair_block * pair_block, axis=0)
        summed_cross, summed_norms = lax.psum((cross, norms), "row")
        rotated = jnp.dot(
            pair_block,
            rotation(summed_norms, summed_cross),
            precision=lax.Precision.HIGHEST,
            preferred_element_type=jnp.float32,
        )
        first_block = rotated[:, :block_width]
        second = rotated[:, block_width:]
        ahead_block = jnp.where(position == 0, second, first_block)
        incoming = from_behind(ahead_block, "pair", 1)
        upcoming = from_behind(second, "pair", -1)
        new_first = jnp.where(position == 0, first_block, incoming)
        new_second = jnp.where(position == pair_count - 1, first_block, upcoming)
        return jnp.concatenate([new_first, new_second], axis=1)

    return lax.fori_loop(0, STEPS, tournament_step, relaid)


def solution(mesh):
    placed = (P(("row", "pair"), None), P())
    return jax.shard_map(
        per_device, mesh=mesh, in_specs=placed, out_specs=P("row", "pair"), check_vma=False
    )
```

profile of v0, /device:TPU:1, one launch (start us, length us, event | category | flops | bytes accessed | tf_op | source)
XLA Modules:
  0.0 842.0 jit_solution(1508597178899747214)
XLA Ops:
  17.2 28.4 %all-to-all-done = f32[256,16,128]{0,2,1:T(8,128)S(1)} async-done(((f32[256,16,128]{0,2,1:T(8,128)}), f32[256,16,128]{0,2,1:T(8,128)S(1)}, u32[]{:S(2)}, u32[]{:S(2)}) %all-to-all-start) | async-done | bytes 2097184 | tf_op jit(solution)/shard_map/all_to_all | solution.py:50
  49.4 790.7 %while.12 = (s32[]{:T(128)}, f32[4096,128]{0,1:T(8,128)S(1)}, pred[]{:T(512)}, pred[]{:T(512)}, s32[]{:T(128)}, /*index=5*/f32[]{:T(128)}) while((s32[]{:T(128)}, f32[4096,128]{0,1:T(8,128)S(1)}, pred[]{:T(512)}, pred[]{:T(512)}, s32[]{:T(128)}, /*index=5*/f32[]{:T(128)}) %tuple.38), condition=%wide.region_5.6_spmd, body=%wide.region_0.5_spmd.sunk | while | flops 1261211776 | bytes 40719056 | solution.py:84
  50.6 28.1 %all-reduce.4 = (f32[64,64]{1,0:T(8,128)S(1)}, f32[128]{0:T(128)S(1)}) all-reduce(f32[64,64]{1,0:T(8,128)S(1)} %fusion.91, f32[128]{0:T(128)S(1)} %multiply_reduce_fusion.4), channel_id=1, replica_groups=mesh['row'=8,'pair'=16] {'row'}, use_global_device_ids=true, to_apply=%region_1.1 | all-reduce | flops 4224 | bytes 33792 | tf_op jit(solution)/shard_map/while/body/eval_jaxpr/psum | solution.py:68
  86.4 12.9 %collective-permute-start = (f32[4096,64]{0,1:T(8,128)S(1)}, f32[4096,64]{0,1:T(8,128)S(1)}, u32[]{:S(2)}, u32[]{:S(2)}) collective-permute-start(f32[4096,64]{0,1:T(8,128)S(1)} %get-tuple-element.113), channel_id=1, source_target_pairs={{0,1},{1,2},{2,3},{3,4},{4,5},{5,6},{6,7},{7,8},{8,9},{9,10},{10,1... | collective-permute-start | bytes 3145736 | tf_op jit(solution)/shard_map/while/body/eval_jaxpr/ppermute | solution.py:15
  101.3 21.6 %collective-permute-done = f32[4096,64]{0,1:T(8,128)S(1)} collective-permute-done((f32[4096,64]{0,1:T(8,128)S(1)}, f32[4096,64]{0,1:T(8,128)S(1)}, u32[]{:S(2)}, u32[]{:S(2)}) %collective-permute-start) | collective-permute-done | bytes 1048608 | tf_op jit(solution)/shard_map/while/body/eval_jaxpr/ppermute | solution.py:15
  126.0 24.4 %all-reduce.4 = (f32[64,64]{1,0:T(8,128)S(1)}, f32[128]{0:T(128)S(1)}) all-reduce(f32[64,64]{1,0:T(8,128)S(1)} %fusion.91, f32[128]{0:T(128)S(1)} %multiply_reduce_fusion.4), channel_id=1, replica_groups=mesh['row'=8,'pair'=16] {'row'}, use_global_device_ids=true, to_apply=%region_1.1 | all-reduce | flops 4224 | bytes 33792 | tf_op jit(solution)/shard_map/while/body/eval_jaxpr/psum | solution.py:68
  158.1 12.8 %collective-permute-start = (f32[4096,64]{0,1:T(8,128)S(1)}, f32[4096,64]{0,1:T(8,128)S(1)}, u32[]{:S(2)}, u32[]{:S(2)}) collective-permute-start(f32[4096,64]{0,1:T(8,128)S(1)} %get-tuple-element.113), channel_id=1, source_target_pairs={{0,1},{1,2},{2,3},{3,4},{4,5},{5,6},{6,7},{7,8},{8,9},{9,10},{10,1... | collective-permute-start | bytes 3145736 | tf_op jit(solution)/shard_map/while/body/eval_jaxpr/ppermute | solution.py:15
  172.8 15.5 %collective-permute-done = f32[4096,64]{0,1:T(8,128)S(1)} collective-permute-done((f32[4096,64]{0,1:T(8,128)S(1)}, f32[4096,64]{0,1:T(8,128)S(1)}, u32[]{:S(2)}, u32[]{:S(2)}) %collective-permute-start) | collective-permute-done | bytes 1048608 | tf_op jit(solution)/shard_map/while/body/eval_jaxpr/ppermute | solution.py:15
  191.9 25.7 %all-reduce.4 = (f32[64,64]{1,0:T(8,128)S(1)}, f32[128]{0:T(128)S(1)}) all-reduce(f32[64,64]{1,0:T(8,128)S(1)} %fusion.91, f32[128]{0:T(128)S(1)} %multiply_reduce_fusion.4), channel_id=1, replica_groups=mesh['row'=8,'pair'=16] {'row'}, use_global_device_ids=true, to_apply=%region_1.1 | all-reduce | flops 4224 | bytes 33792 | tf_op jit(solution)/shard_map/while/body/eval_jaxpr/psum | solution.py:68
  225.4 13.5 %collective-permute-start = (f32[4096,64]{0,1:T(8,128)S(1)}, f32[4096,64]{0,1:T(8,128)S(1)}, u32[]{:S(2)}, u32[]{:S(2)}) collective-permute-start(f32[4096,64]{0,1:T(8,128)S(1)} %get-tuple-element.113), channel_id=1, source_target_pairs={{0,1},{1,2},{2,3},{3,4},{4,5},{5,6},{6,7},{7,8},{8,9},{9,10},{10,1... | collective-permute-start | bytes 3145736 | tf_op jit(solution)/shard_map/while/body/eval_jaxpr/ppermute | solution.py:15
  260.0 24.5 %all-reduce.4 = (f32[64,64]{1,0:T(8,128)S(1)}, f32[128]{0:T(128)S(1)}) all-reduce(f32[64,64]{1,0:T(8,128)S(1)} %fusion.91, f32[128]{0:T(128)S(1)} %multiply_reduce_fusion.4), channel_id=1, replica_groups=mesh['row'=8,'pair'=16] {'row'}, use_global_device_ids=true, to_apply=%region_1.1 | all-reduce | flops 4224 | bytes 33792 | tf_op jit(solution)/shard_map/while/body/eval_jaxpr/psum | solution.py:68
  304.4 16.5 %collective-permute-done = f32[4096,64]{0,1:T(8,128)S(1)} collective-permute-done((f32[4096,64]{0,1:T(8,128)S(1)}, f32[4096,64]{0,1:T(8,128)S(1)}, u32[]{:S(2)}, u32[]{:S(2)}) %collective-permute-start) | collective-permute-done | bytes 1048608 | tf_op jit(solution)/shard_map/while/body/eval_jaxpr/ppermute | solution.py:15
  324.0 25.6 %all-reduce.4 = (f32[64,64]{1,0:T(8,128)S(1)}, f32[128]{0:T(128)S(1)}) all-reduce(f32[64,64]{1,0:T(8,128)S(1)} %fusion.91, f32[128]{0:T(128)S(1)} %multiply_reduce_fusion.4), channel_id=1, replica_groups=mesh['row'=8,'pair'=16] {'row'}, use_global_device_ids=true, to_apply=%region_1.1 | all-reduce | flops 4224 | bytes 33792 | tf_op jit(solution)/shard_map/while/body/eval_jaxpr/psum | solution.py:68
  357.4 13.7 %collective-permute-start = (f32[4096,64]{0,1:T(8,128)S(1)}, f32[4096,64]{0,1:T(8,128)S(1)}, u32[]{:S(2)}, u32[]{:S(2)}) collective-permute-start(f32[4096,64]{0,1:T(8,128)S(1)} %get-tuple-element.113), channel_id=1, source_target_pairs={{0,1},{1,2},{2,3},{3,4},{4,5},{5,6},{6,7},{7,8},{8,9},{9,10},{10,1... | collective-permute-start | bytes 3145736 | tf_op jit(solution)/shard_map/while/body/eval_jaxpr/ppermute | solution.py:15
  373.0 13.2 %collective-permute-done = f32[4096,64]{0,1:T(8,128)S(1)} collective-permute-done((f32[4096,64]{0,1:T(8,128)S(1)}, f32[4096,64]{0,1:T(8,128)S(1)}, u32[]{:S(2)}, u32[]{:S(2)}) %collective-permute-start) | collective-permute-done | bytes 1048608 | tf_op jit(solution)/shard_map/while/body/eval_jaxpr/ppermute | solution.py:15
  392.3 24.5 %all-reduce.4 = (f32[64,64]{1,0:T(8,128)S(1)}, f32[128]{0:T(128)S(1)}) all-reduce(f32[64,64]{1,0:T(8,128)S(1)} %fusion.91, f32[128]{0:T(128)S(1)} %multiply_reduce_fusion.4), channel_id=1, replica_groups=mesh['row'=8,'pair'=16] {'row'}, use_global_device_ids=true, to_apply=%region_1.1 | all-reduce | flops 4224 | bytes 33792 | tf_op jit(solution)/shard_map/while/body/eval_jaxpr/psum | solution.py:68
  436.8 17.4 %collective-permute-done = f32[4096,64]{0,1:T(8,128)S(1)} collective-permute-done((f32[4096,64]{0,1:T(8,128)S(1)}, f32[4096,64]{0,1:T(8,128)S(1)}, u32[]{:S(2)}, u32[]{:S(2)}) %collective-permute-start) | collective-permute-done | bytes 1048608 | tf_op jit(solution)/shard_map/while/body/eval_jaxpr/ppermute | solution.py:15
  457.3 26.4 %all-reduce.4 = (f32[64,64]{1,0:T(8,128)S(1)}, f32[128]{0:T(128)S(1)}) all-reduce(f32[64,64]{1,0:T(8,128)S(1)} %fusion.91, f32[128]{0:T(128)S(1)} %multiply_reduce_fusion.4), channel_id=1, replica_groups=mesh['row'=8,'pair'=16] {'row'}, use_global_device_ids=true, to_apply=%region_1.1 | all-reduce | flops 4224 | bytes 33792 | tf_op jit(solution)/shard_map/while/body/eval_jaxpr/psum | solution.py:68
  491.4 13.4 %collective-permute-start = (f32[4096,64]{0,1:T(8,128)S(1)}, f32[4096,64]{0,1:T(8,128)S(1)}, u32[]{:S(2)}, u32[]{:S(2)}) collective-permute-start(f32[4096,64]{0,1:T(8,128)S(1)} %get-tuple-element.113), channel_id=1, source_target_pairs={{0,1},{1,2},{2,3},{3,4},{4,5},{5,6},{6,7},{7,8},{8,9},{9,10},{10,1... | collective-permute-start | bytes 3145736 | tf_op jit(solution)/shard_map/while/body/eval_jaxpr/ppermute | solution.py:15
  526.2 24.4 %all-reduce.4 = (f32[64,64]{1,0:T(8,128)S(1)}, f32[128]{0:T(128)S(1)}) all-reduce(f32[64,64]{1,0:T(8,128)S(1)} %fusion.91, f32[128]{0:T(128)S(1)} %multiply_reduce_fusion.4), channel_id=1, replica_groups=mesh['row'=8,'pair'=16] {'row'}, use_global_device_ids=true, to_apply=%region_1.1 | all-reduce | flops 4224 | bytes 33792 | tf_op jit(solution)/shard_map/while/body/eval_jaxpr/psum | solution.py:68
  588.2 25.4 %all-reduce.4 = (f32[64,64]{1,0:T(8,128)S(1)}, f32[128]{0:T(128)S(1)}) all-reduce(f32[64,64]{1,0:T(8,128)S(1)} %fusion.91, f32[128]{0:T(128)S(1)} %multiply_reduce_fusion.4), channel_id=1, replica_groups=mesh['row'=8,'pair'=16] {'row'}, use_global_device_ids=true, to_apply=%region_1.1 | all-reduce | flops 4224 | bytes 33792 | tf_op jit(solution)/shard_map/while/body/eval_jaxpr/psum | solution.py:68
  652.5 24.4 %all-reduce.4 = (f32[64,64]{1,0:T(8,128)S(1)}, f32[128]{0:T(128)S(1)}) all-reduce(f32[64,64]{1,0:T(8,128)S(1)} %fusion.91, f32[128]{0:T(128)S(1)} %multiply_reduce_fusion.4), channel_id=1, replica_groups=mesh['row'=8,'pair'=16] {'row'}, use_global_device_ids=true, to_apply=%region_1.1 | all-reduce | flops 4224 | bytes 33792 | tf_op jit(solution)/shard_map/while/body/eval_jaxpr/psum | solution.py:68
  715.0 24.6 %all-reduce.4 = (f32[64,64]{1,0:T(8,128)S(1)}, f32[128]{0:T(128)S(1)}) all-reduce(f32[64,64]{1,0:T(8,128)S(1)} %fusion.91, f32[128]{0:T(128)S(1)} %multiply_reduce_fusion.4), channel_id=1, replica_groups=mesh['row'=8,'pair'=16] {'row'}, use_global_device_ids=true, to_apply=%region_1.1 | all-reduce | flops 4224 | bytes 33792 | tf_op jit(solution)/shard_map/while/body/eval_jaxpr/psum | solution.py:68
  779.2 24.4 %all-reduce.4 = (f32[64,64]{1,0:T(8,128)S(1)}, f32[128]{0:T(128)S(1)}) all-reduce(f32[64,64]{1,0:T(8,128)S(1)} %fusion.91, f32[128]{0:T(128)S(1)} %multiply_reduce_fusion.4), channel_id=1, replica_groups=mesh['row'=8,'pair'=16] {'row'}, use_global_device_ids=true, to_apply=%region_1.1 | all-reduce | flops 4224 | bytes 33792 | tf_op jit(solution)/shard_map/while/body/eval_jaxpr/psum | solution.py:68
  (327 shorter events, 350.3 us)
Async XLA Ops:
  8.8 36.9 %all-to-all-start = ((f32[256,16,128]{0,2,1:T(8,128)}), f32[256,16,128]{0,2,1:T(8,128)S(1)}, u32[]{:S(2)}, u32[]{:S(2)}) async-start(f32[256,16,128]{0,2,1:T(8,128)} %broadcast_select_fusion), calls=%async_computation | async-start | bytes 4194304 | tf_op jit(solution)/shard_map/all_to_all | solution.py:50
  86.4 36.5 %collective-permute-start = (f32[4096,64]{0,1:T(8,128)S(1)}, f32[4096,64]{0,1:T(8,128)S(1)}, u32[]{:S(2)}, u32[]{:S(2)}) collective-permute-start(f32[4096,64]{0,1:T(8,128)S(1)} %get-tuple-element.113), channel_id=1, source_target_pairs={{0,1},{1,2},{2,3},{3,4},{4,5},{5,6},{6,7},{7,8},{8,9},{9,10},{10,1... | collective-permute-start | bytes 3145736 | tf_op jit(solution)/shard_map/while/body/eval_jaxpr/ppermute | solution.py:15
  99.4 23.5 %collective-permute-start.1 = (f32[4096,64]{0,1:T(8,128)S(1)}, f32[4096,64]{0,1:T(8,128)}, u32[]{:S(2)}, u32[]{:S(2)}) collective-permute-start(f32[4096,64]{0,1:T(8,128)S(1)} %get-tuple-element.114), channel_id=1, source_target_pairs={{1,0},{2,1},{3,2},{4,3},{5,4},{6,5},{7,6},{8,7},{9,8},{10,9},{11,1... | collective-permute-start | bytes 3145736 | tf_op jit(solution)/shard_map/while/body/eval_jaxpr/ppermute | solution.py:15
  158.1 30.3 %collective-permute-start = (f32[4096,64]{0,1:T(8,128)S(1)}, f32[4096,64]{0,1:T(8,128)S(1)}, u32[]{:S(2)}, u32[]{:S(2)}) collective-permute-start(f32[4096,64]{0,1:T(8,128)S(1)} %get-tuple-element.113), channel_id=1, source_target_pairs={{0,1},{1,2},{2,3},{3,4},{4,5},{5,6},{6,7},{7,8},{8,9},{9,10},{10,1... | collective-permute-start | bytes 3145736 | tf_op jit(solution)/shard_map/while/body/eval_jaxpr/ppermute | solution.py:15
  170.9 17.9 %collective-permute-start.1 = (f32[4096,64]{0,1:T(8,128)S(1)}, f32[4096,64]{0,1:T(8,128)}, u32[]{:S(2)}, u32[]{:S(2)}) collective-permute-start(f32[4096,64]{0,1:T(8,128)S(1)} %get-tuple-element.114), channel_id=1, source_target_pairs={{1,0},{2,1},{3,2},{4,3},{5,4},{6,5},{7,6},{8,7},{9,8},{10,9},{11,1... | collective-permute-start | bytes 3145736 | tf_op jit(solution)/shard_map/while/body/eval_jaxpr/ppermute | solution.py:15
  225.4 27.6 %collective-permute-start = (f32[4096,64]{0,1:T(8,128)S(1)}, f32[4096,64]{0,1:T(8,128)S(1)}, u32[]{:S(2)}, u32[]{:S(2)}) collective-permute-start(f32[4096,64]{0,1:T(8,128)S(1)} %get-tuple-element.113), channel_id=1, source_target_pairs={{0,1},{1,2},{2,3},{3,4},{4,5},{5,6},{6,7},{7,8},{8,9},{9,10},{10,1... | collective-permute-start | bytes 3145736 | tf_op jit(solution)/shard_map/while/body/eval_jaxpr/ppermute | solution.py:15
  238.8 18.1 %collective-permute-start.1 = (f32[4096,64]{0,1:T(8,128)S(1)}, f32[4096,64]{0,1:T(8,128)}, u32[]{:S(2)}, u32[]{:S(2)}) collective-permute-start(f32[4096,64]{0,1:T(8,128)S(1)} %get-tuple-element.114), channel_id=1, source_target_pairs={{1,0},{2,1},{3,2},{4,3},{5,4},{6,5},{7,6},{8,7},{9,8},{10,9},{11,1... | collective-permute-start | bytes 3145736 | tf_op jit(solution)/shard_map/while/body/eval_jaxpr/ppermute | solution.py:15
  292.2 28.6 %collective-permute-start = (f32[4096,64]{0,1:T(8,128)S(1)}, f32[4096,64]{0,1:T(8,128)S(1)}, u32[]{:S(2)}, u32[]{:S(2)}) collective-permute-start(f32[4096,64]{0,1:T(8,128)S(1)} %get-tuple-element.113), channel_id=1, source_target_pairs={{0,1},{1,2},{2,3},{3,4},{4,5},{5,6},{6,7},{7,8},{8,9},{9,10},{10,1... | collective-permute-start | bytes 3145736 | tf_op jit(solution)/shard_map/while/body/eval_jaxpr/ppermute | solution.py:15
  302.4 18.5 %collective-permute-start.1 = (f32[4096,64]{0,1:T(8,128)S(1)}, f32[4096,64]{0,1:T(8,128)}, u32[]{:S(2)}, u32[]{:S(2)}) collective-permute-start(f32[4096,64]{0,1:T(8,128)S(1)} %get-tuple-element.114), channel_id=1, source_target_pairs={{1,0},{2,1},{3,2},{4,3},{5,4},{6,5},{7,6},{8,7},{9,8},{10,9},{11,1... | collective-permute-start | bytes 3145736 | tf_op jit(solution)/shard_map/while/body/eval_jaxpr/ppermute | solution.py:15
  357.4 28.9 %collective-permute-start = (f32[4096,64]{0,1:T(8,128)S(1)}, f32[4096,64]{0,1:T(8,128)S(1)}, u32[]{:S(2)}, u32[]{:S(2)}) collective-permute-start(f32[4096,64]{0,1:T(8,128)S(1)} %get-tuple-element.113), channel_id=1, source_target_pairs={{0,1},{1,2},{2,3},{3,4},{4,5},{5,6},{6,7},{7,8},{8,9},{9,10},{10,1... | collective-permute-start | bytes 3145736 | tf_op jit(solution)/shard_map/while/body/eval_jaxpr/ppermute | solution.py:15
  371.1 18.1 %collective-permute-start.1 = (f32[4096,64]{0,1:T(8,128)S(1)}, f32[4096,64]{0,1:T(8,128)}, u32[]{:S(2)}, u32[]{:S(2)}) collective-permute-start(f32[4096,64]{0,1:T(8,128)S(1)} %get-tuple-element.114), channel_id=1, source_target_pairs={{1,0},{2,1},{3,2},{4,3},{5,4},{6,5},{7,6},{8,7},{9,8},{10,9},{11,1... | collective-permute-start | bytes 3145736 | tf_op jit(solution)/shard_map/while/body/eval_jaxpr/ppermute | solution.py:15
  424.5 29.7 %collective-permute-start = (f32[4096,64]{0,1:T(8,128)S(1)}, f32[4096,64]{0,1:T(8,128)S(1)}, u32[]{:S(2)}, u32[]{:S(2)}) collective-permute-start(f32[4096,64]{0,1:T(8,128)S(1)} %get-tuple-element.113), channel_id=1, source_target_pairs={{0,1},{1,2},{2,3},{3,4},{4,5},{5,6},{6,7},{7,8},{8,9},{9,10},{10,1... | collective-permute-start | bytes 3145736 | tf_op jit(solution)/shard_map/while/body/eval_jaxpr/ppermute | solution.py:15
  434.8 19.4 %collective-permute-start.1 = (f32[4096,64]{0,1:T(8,128)S(1)}, f32[4096,64]{0,1:T(8,128)}, u32[]{:S(2)}, u32[]{:S(2)}) collective-permute-start(f32[4096,64]{0,1:T(8,128)S(1)} %get-tuple-element.114), channel_id=1, source_target_pairs={{1,0},{2,1},{3,2},{4,3},{5,4},{6,5},{7,6},{8,7},{9,8},{10,9},{11,1... | collective-permute-start | bytes 3145736 | tf_op jit(solution)/shard_map/while/body/eval_jaxpr/ppermute | solution.py:15
  491.4 27.0 %collective-permute-start = (f32[4096,64]{0,1:T(8,128)S(1)}, f32[4096,64]{0,1:T(8,128)S(1)}, u32[]{:S(2)}, u32[]{:S(2)}) collective-permute-start(f32[4096,64]{0,1:T(8,128)S(1)} %get-tuple-element.113), channel_id=1, source_target_pairs={{0,1},{1,2},{2,3},{3,4},{4,5},{5,6},{6,7},{7,8},{8,9},{9,10},{10,1... | collective-permute-start | bytes 3145736 | tf_op jit(solution)/shard_map/while/body/eval_jaxpr/ppermute | solution.py:15
  504.8 18.2 %collective-permute-start.1 = (f32[4096,64]{0,1:T(8,128)S(1)}, f32[4096,64]{0,1:T(8,128)}, u32[]{:S(2)}, u32[]{:S(2)}) collective-permute-start(f32[4096,64]{0,1:T(8,128)S(1)} %get-tuple-element.114), channel_id=1, source_target_pairs={{1,0},{2,1},{3,2},{4,3},{5,4},{6,5},{7,6},{8,7},{9,8},{10,9},{11,1... | collective-permute-start | bytes 3145736 | tf_op jit(solution)/shard_map/while/body/eval_jaxpr/ppermute | solution.py:15
  558.3 22.7 %collective-permute-start = (f32[4096,64]{0,1:T(8,128)S(1)}, f32[4096,64]{0,1:T(8,128)S(1)}, u32[]{:S(2)}, u32[]{:S(2)}) collective-permute-start(f32[4096,64]{0,1:T(8,128)S(1)} %get-tuple-element.113), channel_id=1, source_target_pairs={{0,1},{1,2},{2,3},{3,4},{4,5},{5,6},{6,7},{7,8},{8,9},{9,10},{10,1... | collective-permute-start | bytes 3145736 | tf_op jit(solution)/shard_map/while/body/eval_jaxpr/ppermute | solution.py:15
  567.0 18.1 %collective-permute-start.1 = (f32[4096,64]{0,1:T(8,128)S(1)}, f32[4096,64]{0,1:T(8,128)}, u32[]{:S(2)}, u32[]{:S(2)}) collective-permute-start(f32[4096,64]{0,1:T(8,128)S(1)} %get-tuple-element.114), channel_id=1, source_target_pairs={{1,0},{2,1},{3,2},{4,3},{5,4},{6,5},{7,6},{8,7},{9,8},{10,9},{11,1... | collective-permute-start | bytes 3145736 | tf_op jit(solution)/shard_map/while/body/eval_jaxpr/ppermute | solution.py:15
  621.4 23.8 %collective-permute-start = (f32[4096,64]{0,1:T(8,128)S(1)}, f32[4096,64]{0,1:T(8,128)S(1)}, u32[]{:S(2)}, u32[]{:S(2)}) collective-permute-start(f32[4096,64]{0,1:T(8,128)S(1)} %get-tuple-element.113), channel_id=1, source_target_pairs={{0,1},{1,2},{2,3},{3,4},{4,5},{5,6},{6,7},{7,8},{8,9},{9,10},{10,1... | collective-permute-start | bytes 3145736 | tf_op jit(solution)/shard_map/while/body/eval_jaxpr/ppermute | solution.py:15
  631.3 18.1 %collective-permute-start.1 = (f32[4096,64]{0,1:T(8,128)S(1)}, f32[4096,64]{0,1:T(8,128)}, u32[]{:S(2)}, u32[]{:S(2)}) collective-permute-start(f32[4096,64]{0,1:T(8,128)S(1)} %get-tuple-element.114), channel_id=1, source_target_pairs={{1,0},{2,1},{3,2},{4,3},{5,4},{6,5},{7,6},{8,7},{9,8},{10,9},{11,1... | collective-permute-start | bytes 3145736 | tf_op jit(solution)/shard_map/while/body/eval_jaxpr/ppermute | solution.py:15
  684.7 23.1 %collective-permute-start = (f32[4096,64]{0,1:T(8,128)S(1)}, f32[4096,64]{0,1:T(8,128)S(1)}, u32[]{:S(2)}, u32[]{:S(2)}) collective-permute-start(f32[4096,64]{0,1:T(8,128)S(1)} %get-tuple-element.113), channel_id=1, source_target_pairs={{0,1},{1,2},{2,3},{3,4},{4,5},{5,6},{6,7},{7,8},{8,9},{9,10},{10,1... | collective-permute-start | bytes 3145736 | tf_op jit(solution)/shard_map/while/body/eval_jaxpr/ppermute | solution.py:15
  693.8 18.1 %collective-permute-start.1 = (f32[4096,64]{0,1:T(8,128)S(1)}, f32[4096,64]{0,1:T(8,128)}, u32[]{:S(2)}, u32[]{:S(2)}) collective-permute-start(f32[4096,64]{0,1:T(8,128)S(1)} %get-tuple-element.114), channel_id=1, source_target_pairs={{1,0},{2,1},{3,2},{4,3},{5,4},{6,5},{7,6},{8,7},{9,8},{10,9},{11,1... | collective-permute-start | bytes 3145736 | tf_op jit(solution)/shard_map/while/body/eval_jaxpr/ppermute | solution.py:15
  747.3 24.6 %collective-permute-start = (f32[4096,64]{0,1:T(8,128)S(1)}, f32[4096,64]{0,1:T(8,128)S(1)}, u32[]{:S(2)}, u32[]{:S(2)}) collective-permute-start(f32[4096,64]{0,1:T(8,128)S(1)} %get-tuple-element.113), channel_id=1, source_target_pairs={{0,1},{1,2},{2,3},{3,4},{4,5},{5,6},{6,7},{7,8},{8,9},{9,10},{10,1... | collective-permute-start | bytes 3145736 | tf_op jit(solution)/shard_map/while/body/eval_jaxpr/ppermute | solution.py:15
  758.0 18.1 %collective-permute-start.1 = (f32[4096,64]{0,1:T(8,128)S(1)}, f32[4096,64]{0,1:T(8,128)}, u32[]{:S(2)}, u32[]{:S(2)}) collective-permute-start(f32[4096,64]{0,1:T(8,128)S(1)} %get-tuple-element.114), channel_id=1, source_target_pairs={{1,0},{2,1},{3,2},{4,3},{5,4},{6,5},{7,6},{8,7},{9,8},{10,9},{11,1... | collective-permute-start | bytes 3145736 | tf_op jit(solution)/shard_map/while/body/eval_jaxpr/ppermute | solution.py:15
  811.4 23.0 %collective-permute-start = (f32[4096,64]{0,1:T(8,128)S(1)}, f32[4096,64]{0,1:T(8,128)S(1)}, u32[]{:S(2)}, u32[]{:S(2)}) collective-permute-start(f32[4096,64]{0,1:T(8,128)S(1)} %get-tuple-element.113), channel_id=1, source_target_pairs={{0,1},{1,2},{2,3},{3,4},{4,5},{5,6},{6,7},{7,8},{8,9},{9,10},{10,1... | collective-permute-start | bytes 3145736 | tf_op jit(solution)/shard_map/while/body/eval_jaxpr/ppermute | solution.py:15
  (13 other events, 33.6 us)
where the time goes:
time: 844 us; the launch traced here: 842 us
  blocking collectives  302 us (36%)
  waiting for transfers between devices  229 us (27%)
  starting transfers between devices  166 us (20%)
  matrix products  68.3 us (8%)
  other arithmetic  41.5 us (5%)
  local copies, waits for them, and re-layouts  24.5 us (3%)
  loops' own time  10.1 us (1%)
    psum x12, blocking collectives, tournament_step(): summed_cross, summed_norms = lax.psum((cross, norms), 'row')  302 us
    ppermute x24, waiting for transfers between devices, from_behind(): return lax.ppermute(block, axis, route)  201 us
    ppermute x24, starting transfers between devices, from_behind(): return lax.ppermute(block, axis, route)  158 us
    dot_general x120, matrix products, matmul_high(): return jnp.matmul(left, right, precision=lax.Precision.HIGHEST)  33.3 us
    all_to_all x1, waiting for transfers between devices, per_device(): lax.all_to_all(arranged.reshape(row_count, block_count * block_width), 'p...  28.4 us
    dot_general x12, matrix products, tournament_step(): jnp.dot(pair_block, rotation(summed_norms, summed_cross), precision=lax.P...  23.2 us
    select_n x12, other arithmetic, tournament_step(): new_first = jnp.where(position == 0, first_block, incoming)  20.6 us
  transfers between devices with their start and end apart: 25, of which 22 were waited for; matrix products, arithmetic and copies ran while one was open for 0% of the time, Pallas kernels for 0%

commit v1 on v0

v1 whole, which is shorter than its diff:
```python
import math

import jax
import jax.numpy as jnp
from jax import lax
from jax.experimental import pallas as pl
from jax.experimental.pallas import tpu as pltpu
from jax.sharding import PartitionSpec as P

STEPS = 12
CHIPS = 8
SLOTS = 8
WIDTH = 64
PART = 40
MESH = pl.DeviceIdType.MESH
BF = jnp.bfloat16
F32 = jnp.float32
NT = (((1,), (1,)), ((), ()))


def split(x):
    high = x.astype(BF)
    return high, (x - high.astype(F32)).astype(BF)


def product(left, right):
    wide = jnp.concatenate(right, axis=1)
    y = jnp.dot(
        jnp.concatenate(left, axis=1), jnp.concatenate([wide, wide], axis=0), preferred_element_type=F32
    )
    return y[:, 0:128] + y[:, 128:256]


def tree(pieces):
    while len(pieces) > 1:
        pieces = [a + b for a, b in zip(pieces[::2], pieces[1::2])]
    return pieces[0]


def kernel(
    order_ref, xt_ref, out_ref,
    first0, first1, second0, second1, export, arrive, outbox, inbox, part, gather1, gather2, total, turn, final,
    send1, recv1, send2, recv2, send3, recv3, sendx, recvx, sendb, recvb, sendf, recvf,
):
    row = lax.axis_index("row")
    pair = lax.axis_index("pair")
    z, y_low = row // 2, row % 2
    chip, core = pair // 2, pair % 2
    x, y_high = chip // 2, chip % 2
    side = (y_low + y_high) % 2
    sibling = pair + 1 - 2 * core
    firsts, seconds = (first0, first1), (second0, second1)
    me1 = x * 2 + side
    me2 = z * 2 + y_high

    def sharer(j):
        return (z * 2 + (j + y_high) % 2, ((j // 2) * 2 + y_high) * 2 + core)

    def holder(j):
        return ((j // 2) * 2 + (side + j) % 2, (x * 2 + j % 2) * 2 + core)

    lanes = xt_ref.shape[2]
    here = pl.ds(pl.multiple_of(core * lanes, lanes), lanes)
    there = pl.ds(pl.multiple_of((1 - core) * lanes, lanes), lanes)

    barrier = pltpu.get_barrier_semaphore()

    def greet(device):
        pl.semaphore_signal(barrier, inc=1, device_id=device, device_id_type=MESH)

    for d in range(1, 8):
        greet(sharer((me1 + d) % 8))
        greet(holder((me2 + d) % 8))
    for d in range(1, 2 * CHIPS):
        greet((row, (pair + d) % (2 * CHIPS)))

    def position(owner, block):
        plain = 2 * (block % SLOTS) + block // SLOTS
        return plain + owner * (31 - 2 * plain)

    for b in range(2 * SLOTS):
        outbox[b] = xt_ref[order_ref[position(1 - core, b)]]
    pl.semaphore_wait(barrier, 14 + 2 * CHIPS - 1)
    swap = pltpu.make_async_remote_copy(
        src_ref=outbox, dst_ref=inbox, send_sem=sendb, recv_sem=recvb,
        device_id=(row, sibling), device_id_type=MESH,
    )
    swap.start()
    for b in range(2 * SLOTS):
        high, low = split(xt_ref[order_ref[position(core, b)]])
        state = first0 if b < SLOTS else second0
        state[b % SLOTS, 0:WIDTH, here] = high
        state[b % SLOTS, WIDTH:, here] = low
    swap.wait()
    for b in range(2 * SLOTS):
        high, low = split(inbox[b])
        state = first0 if b < SLOTS else second0
        state[b % SLOTS, 0:WIDTH, there] = high
        state[b % SLOTS, WIDTH:, there] = low

    lane32 = lax.broadcasted_iota(jnp.int32, (32, 128), 1)
    lane64 = lax.broadcasted_iota(jnp.int32, (64, 128), 1)
    sub64 = lax.broadcasted_iota(jnp.int32, (64, 128), 0)
    unit = (
        lax.broadcasted_iota(jnp.int32, (128, 128), 0)
        == lax.broadcasted_iota(jnp.int32, (128, 128), 1)
    ).astype(F32)
    ones = jnp.ones((8, 256), BF)
    minus_sign = (2 * core - 1).astype(F32)

    def bulk(buffer, sem):
        return pltpu.make_async_copy(buffer, buffer, sem)

    def crossing(now, j):
        a = firsts[now][j]
        b = seconds[now][j]
        grown = lax.dot_general(a, b, NT, preferred_element_type=F32)
        grown = grown[0:64] + grown[64:128]
        both = grown + pltpu.roll(grown, 64, 1)
        part[now, j, 0:32] = jnp.where(lane32 < 64, both[0:32], both[32:64])
        squares = []
        for v in (a, b):
            u = v[0:64].astype(F32) + v[64:128].astype(F32)
            u = u * u
            squares.append(u[:, 0:128] + u[:, 128:256] + (u[:, 256:384] + u[:, 384:512]))
        squares = jnp.concatenate(split(jnp.concatenate(squares, axis=0)), axis=1)
        part[now, j, 32:40] = lax.dot_general(ones, squares, NT, preferred_element_type=F32)

    def send_parts(now):
        for d in range(1, 8):
            j = (me1 + d) % 8
            pltpu.make_async_remote_copy(
                src_ref=part.at[now, j], dst_ref=gather1.at[now, me1],
                send_sem=send1.at[now], recv_sem=recv1.at[now],
                device_id=sharer(j), device_id_type=MESH,
            ).start()
        gather1[now, me1] = part[now, me1]

    def rotations(now):
        bulk(gather1.at[now, pl.ds(0, 7)], recv1.at[now]).wait()
        gather2[now, me2] = tree([gather1[now, s] for s in range(8)])
        for d in range(1, 8):
            pltpu.make_async_remote_copy(
                src_ref=gather2.at[now, me2], dst_ref=gather2.at[now, me2],
                send_sem=send2.at[now], recv_sem=recv2.at[now],
                device_id=holder((me2 + d) % 8), device_id_type=MESH,
            ).start()
        bulk(gather2.at[now, pl.ds(0, 7)], recv2.at[now]).wait()
        total[now, me1] = tree([gather2[now, s] for s in range(8)])
        for d in range(1, 8):
            pltpu.make_async_remote_copy(
                src_ref=total.at[now, me1], dst_ref=total.at[now, me1],
                send_sem=send3.at[now], recv_sem=recv3.at[now],
                device_id=sharer((me1 + d) % 8), device_id_type=MESH,
            ).start()
        bulk(total.at[now, pl.ds(0, 7)], recv3.at[now]).wait()
        bulk(part.at[now, pl.ds(0, 7)], send1.at[now]).wait()
        bulk(gather2.at[now, pl.ds(0, 7)], send2.at[now]).wait()
        bulk(total.at[now, pl.ds(0, 7)], send3.at[now]).wait()

        skews = []
        for j in range(SLOTS):
            packed = total[now, j, 0:32]
            inverse = lax.rsqrt(total[now, j, 32:40] + 1e-06)[0:1]
            turned = pltpu.roll(packed, 64, 1)
            cross = jnp.concatenate(
                [jnp.where(lane32 < 64, packed, turned), jnp.where(lane32 < 64, turned, packed)], axis=0
            )
            column = jnp.sum(jnp.where(lane64 == sub64, inverse, 0.0), axis=1, keepdims=True)
            cosine = jnp.where(lane64 >= 64, cross * inverse, 0.0) * column
            frobenius = jnp.sqrt(jnp.sum(cosine * cosine, axis=(0, 1), keepdims=True))
            upper = jnp.concatenate([cosine * (minus_sign / (1.0 + frobenius)), jnp.zeros((64, 128), F32)], axis=0)
            skews.append(upper - upper.T)
        e0, w0, e1, w1, e2 = [], [], [], [], []
        for k in skews:
            high, low = split(k)
            m = lax.dot_general(
                jnp.concatenate([high, low], axis=1),
                jnp.concatenate(
                    [jnp.concatenate([high, high], axis=1), jnp.concatenate([low, low], axis=1)], axis=0
                ),
                NT, preferred_element_type=F32,
            )
            e0.append(0.5 * (unit - (m[:, 0:128] + m[:, 128:256])))
        for j in range(SLOTS):
            parts = split(e0[j])
            e1.append((product(parts, parts), 0.75 * unit + 0.25 * e0[j]))
            w0.append(product(split(unit + skews[j]), split(unit + 0.5 * e0[j])))
        e1 = [product(split(a), split(b)) for a, b in e1]
        for j in range(SLOTS):
            parts = split(e1[j])
            e2.append((product(parts, parts), 0.75 * unit + 0.25 * e1[j]))
            w1.append(product(split(w0[j]), split(unit + 0.5 * e1[j])))
        e2 = [product(split(a), split(b)) for a, b in e2]
        for j in range(SLOTS):
            r = product(split(w1[j]), split(unit + 0.5 * e2[j])) * (1.0 / math.sqrt(2.0))
            high, low = split(r)
            turn[j, :, 0:128] = high
            turn[j, :, 128:256] = low
            turn[j, :, 256:384] = high

    def apply(now, j):
        a, b = firsts[now], seconds[now]
        high = jnp.concatenate([a[j, 0:WIDTH], b[j, 0:WIDTH]], axis=0)
        low = jnp.concatenate([a[j, WIDTH:], b[j, WIDTH:]], axis=0)
        r = jnp.dot(turn[j], jnp.concatenate([high, high, low], axis=0), preferred_element_type=F32)
        return r[0:WIDTH], r[WIDTH:]

    def put(state, j, v):
        high, low = split(v)
        state[j, 0:WIDTH] = high
        state[j, WIDTH:] = low

    def advance(now):
        later = 1 - now
        first, second = firsts[later], seconds[later]
        a, b = apply(now, SLOTS - 1)
        export[now] = a
        swap = pltpu.make_async_remote_copy(
            src_ref=export.at[now], dst_ref=arrive.at[now],
            send_sem=sendx.at[now], recv_sem=recvx.at[now],
            device_id=(row, sibling), device_id_type=MESH,
        )
        swap.start()
        put(second, SLOTS - 2, b)
        a, b = apply(now, 0)
        put(first, core, a)
        put(first, 1 - core, b)
        for j in range(1, SLOTS - 1):
            a, b = apply(now, j)
            put(first, j + 1, a)
            put(second, j - 1, b)
        for j in range(SLOTS - 1):
            crossing(later, j)
        swap.wait()
        put(second, SLOTS - 1, arrive[now])
        crossing(later, SLOTS - 1)
        send_parts(later)

    def finish():
        for j in range(SLOTS):
            a, b = apply(1, j)
            final[2 * core if j == 0 else min(2 * j + 2, 15)] = a
            final[2 - 2 * core if j == 0 else 2 * j - 1] = b

        def place(d):
            m = ((chip % 4) * 4 + d) % 16
            n = m + m // 15
            n = n + core * (31 - 2 * n)
            return m, n // 2, n % 2

        def start(d, carry):
            m, owner, half = place(d)
            target = out_ref.at[chip, pl.ds(pl.multiple_of(half * WIDTH, WIDTH), WIDTH)]
            arrived = recvf.at[chip, half]

            @pl.when(owner != pair)
            def _():
                pltpu.make_async_remote_copy(
                    src_ref=final.at[m], dst_ref=target, send_sem=sendf.at[m], recv_sem=arrived,
                    device_id=(row, owner), device_id_type=MESH,
                ).start()

            @pl.when(owner == pair)
            def _():
                pltpu.make_async_copy(final.at[m], target, arrived).start()

            return carry

        lax.fori_loop(0, 16, start, 0)

        def sent(d, carry):
            m, owner, half = place(d)

            @pl.when(owner != pair)
            def _():
                bulk(final.at[m], sendf.at[m]).wait()

            return carry

        lax.fori_loop(0, 16, sent, 0)
        for c in range(CHIPS):
            for half in range(2):
                bulk(out_ref.at[c, pl.ds(half * WIDTH, WIDTH)], recvf.at[c, half]).wait()

    for j in range(SLOTS):
        crossing(0, j)
    send_parts(0)

    def two_steps(i, carry):
        rotations(0)
        advance(0)
        rotations(1)

        @pl.when(i < STEPS // 2 - 1)
        def _():
            advance(1)

        @pl.when(i == STEPS // 2 - 1)
        def _():
            finish()

        return carry

    lax.fori_loop(0, STEPS // 2, two_steps, 0)


def per_device(snapshots, start_order):
    rows = snapshots.shape[0]
    wide = 2 * rows
    transposed = snapshots.T.reshape(4 * SLOTS, WIDTH, rows)
    dma = pltpu.SemaphoreType.DMA
    blocks = pl.pallas_call(
        kernel,
        out_shape=jax.ShapeDtypeStruct((CHIPS, 2 * WIDTH, wide), F32),
        in_specs=[pl.BlockSpec(memory_space=pltpu.SMEM), pl.BlockSpec(memory_space=pltpu.VMEM)],
        out_specs=pl.BlockSpec(memory_space=pl.ANY),
        scratch_shapes=[
            pltpu.VMEM((SLOTS, 2 * WIDTH, wide), BF),
            pltpu.VMEM((SLOTS, 2 * WIDTH, wide), BF),
            pltpu.VMEM((SLOTS, 2 * WIDTH, wide), BF),
            pltpu.VMEM((SLOTS, 2 * WIDTH, wide), BF),
            pltpu.VMEM((2, WIDTH, wide), F32),
            pltpu.VMEM((2, WIDTH, wide), F32),
            pltpu.VMEM((2 * SLOTS, WIDTH, rows), F32),
            pltpu.VMEM((2 * SLOTS, WIDTH, rows), F32),
            pltpu.VMEM((2, SLOTS, PART, 128), F32),
            pltpu.VMEM((2, 8, PART, 128), F32),
            pltpu.VMEM((2, 8, PART, 128), F32),
            pltpu.VMEM((2, SLOTS, PART, 128), F32),
            pltpu.VMEM((SLOTS, 128, 384), BF),
            pltpu.VMEM((2 * SLOTS, WIDTH, wide), F32),
            dma((2,)), dma((2,)), dma((2,)), dma((2,)), dma((2,)), dma((2,)), dma((2,)), dma((2,)),
            dma(()), dma(()), dma((2 * SLOTS,)), dma((CHIPS, 2)),
        ],
        compiler_params=pltpu.CompilerParams(
            collective_id=0, has_side_effects=True, vmem_limit_bytes=40 * 1024 * 1024
        ),
    )(start_order, transposed)
    return blocks.transpose(0, 2, 1).reshape(CHIPS * wide, 2 * WIDTH)


def solution(mesh):
    placed = (P(("row", "pair"), None), P())
    return jax.shard_map(
        per_device, mesh=mesh, in_specs=placed, out_specs=P("row", "pair"), check_vma=False
    )
```

time: 844 us -> 267 us (0.32)
  blocking collectives: 302 us -> 0 us
  Pallas kernels: 0 us -> 257 us
  waiting for transfers between devices: 229 us -> 0 us
  starting transfers between devices: 166 us -> 0 us
  matrix products: 68.3 us -> 0 us
  other arithmetic: 41.5 us -> 0 us
  local copies, waits for them, and re-layouts: 24.5 us -> 6.3 us
  loops' own time: 10.1 us -> 0 us
    psum x12 -> x0, blocking collectives: 302 us -> none  [tournament_step(): summed_cross, summed_norms = lax.psum((cross, norms), 'row')]
    pallas_call x0 -> x1, Pallas kernels: none -> 257 us  [per_device(): pl.pallas_call(kernel, out_shape=jax.ShapeDtypeStruct((CHIPS, 2 * WIDTH,...]
    ppermute x24 -> x0, waiting for transfers between devices: 201 us -> none  [from_behind(): return lax.ppermute(block, axis, route)]
    ppermute x24 -> x0, starting transfers between devices: 158 us -> none  [from_behind(): return lax.ppermute(block, axis, route)]
    dot_general x144 -> x0, matrix products: 68.3 us -> none  [the longest x120 33.3 us: matmul_high(): return jnp.matmul(left, right, precision=lax.Precision.HIGHEST)]
    all_to_all x1 -> x0, waiting for transfers between devices: 28.4 us -> none  [per_device(): lax.all_to_all(arranged.reshape(row_count, block_count * block_width), 'p...]
    select_n x26 -> x0, other arithmetic: 27.2 us -> none  [the longest x12 20.6 us: tournament_step(): new_first = jnp.where(position == 0, first_block, incoming)]
    while x26 -> x0, local copies, waits for them, and re-layouts: 16.7 us -> none
  transfers between devices with their start and end apart: 25 -> 0, of which waited for: 22 -> 0; matrix products, arithmetic and copies ran while one was open for 0% -> 0% of each run, Pallas kernels for 0% -> 0%
where the time goes in v1:
time: 267 us; the launch traced here: 264 us
  Pallas kernels  257 us (96%)
  local copies, waits for them, and re-layouts  6.3 us (2%)
    pallas_call x1, Pallas kernels, per_device(): pl.pallas_call(kernel, out_shape=jax.ShapeDtypeStruct((CHIPS, 2 * WIDTH,...  257 us

profile of v1, /device:TPU:1, one launch (start us, length us, event | category | flops | bytes accessed | tf_op | source)
XLA Modules:
  0.0 263.6 jit_solution(6813855232678326972)
XLA Ops:
  0.0 0.0 copy-start.1
  0.0 2.9 %copy.4 = f32[2048,256]{1,0:T(8,128)} copy(f32[2048,256]{0,1:T(8,128)} %bitcast.6) | data formatting | bytes 4194304 | tf_op jit(solution)/shard_map/transpose | solution.py:311
  2.9 0.0 copy-done.1
  2.9 0.0 copy-start
  2.9 1.6 copy-done
  4.5 257.3 %shard_map.28 = f32[8,128,512]{2,1,0:T(8,128)S(1)} custom-call(s32[32]{0:T(128)S(1)} %copy-done.1, f32[32,64,256]{2,1,0:T(8,128)S(1)} %bitcast.5), custom_call_target="tpu_custom_call" | custom-call | tf_op jit(solution)/shard_map/pallas_call | solution.py:313
  261.8 1.8 copy.5
Async XLA Ops:
  0.0 2.9 %copy-start.1 = (s32[32]{0:T(128)S(1)}, s32[32]{0:T(128)}, u32[]{:S(2)}) copy-start(s32[32]{0:T(128)} %order_ref.1) | copy-start | bytes 388
  2.9 1.6 copy-start

commit v2 on v1

--- a/solution.py
+++ b/solution.py
@@ -2,6 +2,7 @@
 
 import jax
 import jax.numpy as jnp
+import numpy as np
 from jax import lax
 from jax.experimental import pallas as pl
 from jax.experimental.pallas import tpu as pltpu
@@ -23,12 +24,116 @@
     return high, (x - high.astype(F32)).astype(BF)
 
 
-def product(left, right):
-    wide = jnp.concatenate(right, axis=1)
-    y = jnp.dot(
-        jnp.concatenate(left, axis=1), jnp.concatenate([wide, wide], axis=0), preferred_element_type=F32
+def newton_schulz():
+    e0 = np.polynomial.Polynomial([0.5, -0.5])
+    e1 = e0 * e0 * (0.75 + 0.25 * e0)
+    e2 = e1 * e1 * (0.75 + 0.25 * e1)
+    f = (1 + 0.5 * e0) * (1 + 0.5 * e1) * (1 + 0.5 * e2) / math.sqrt(2.0)
+    g = np.polynomial.Polynomial(f.coef[1:])(np.polynomial.Polynomial([0.5, 1.0]))
+    return float(f.coef[0]), [float(c) for c in g.coef]
+
+
+ORIGIN, SERIES = newton_schulz()
+
+
+def dot3(left, right, dims=(((1,), (0,)), ((), ()))):
+    axis = dims[0][1][0]
+    return lax.dot_general(
+        jnp.concatenate([left[0], left[1], left[0]], axis=1),
+        jnp.concatenate([right[0], right[0], right[1]], axis=axis),
+        dims, preferred_element_type=F32,
     )
-    return y[:, 0:128] + y[:, 128:256]
+
+
+def coupling(sums, sign):
+    lane = lax.broadcasted_iota(jnp.int32, (32, 128), 1)
+    row = lax.broadcasted_iota(jnp.int32, (32, 128), 0)
+    left = lane < 64
+    inverse = lax.rsqrt(sums[32:40] + 1e-06)
+    across = jnp.where(left[0:1], pltpu.roll(inverse, 64, 1)[0:1], inverse[0:1])
+    down = jnp.where(
+        left,
+        jnp.sum(jnp.where(lane == row, inverse[0:1], 0.0), axis=1, keepdims=True),
+        jnp.sum(jnp.where(lane == row + 32, inverse[0:1], 0.0), axis=1, keepdims=True),
+    )
+    cosine = sums[0:32] * across * down
+    frobenius = jnp.sqrt(jnp.sum(cosine * cosine, axis=(0, 1), keepdims=True))
+    return cosine * (sign / (1.0 + frobenius))
+
+
+def turn_matrices(packed):
+    lane32 = lax.broadcasted_iota(jnp.int32, (32, 128), 1) < 64
+    lane = lax.broadcasted_iota(jnp.int32, (64, 128), 1)
+    row = lax.broadcasted_iota(jnp.int32, (64, 128), 0)
+    left = lane < 64
+    right_unit = lane - 64 == row
+    unit = ((lane == row) | right_unit).astype(F32)
+    keep_left, keep_right = left.astype(F32).astype(BF), (1.0 - left.astype(F32)).astype(BF)
+    count = len(packed) // 2
+
+    def swap(v):
+        return pltpu.roll(v, 64, 1)
+
+    def diagonal(v):
+        return jnp.concatenate([v * keep_left, v * keep_right], axis=0)
+
+    def pairs(v):
+        return tuple(diagonal(part) for part in split(v))
+
+    def times(a, b):
+        wide = jnp.concatenate(b, axis=1)
+        y = jnp.dot(
+            jnp.concatenate(split(a), axis=1), jnp.concatenate([wide, wide], axis=0), preferred_element_type=F32
+        )
+        return y[:, 0:128] + y[:, 128:256]
+
+    def once(a, b):
+        return jnp.dot(a.astype(BF), b, preferred_element_type=F32)
+
+    def beside(p, q):
+        none = jnp.zeros((64, 128), BF)
+        parts = []
+        for u, v in zip(split(p), split(q)):
+            parts.append(
+                jnp.concatenate([jnp.concatenate([u, none], axis=1), jnp.concatenate([none, v], axis=1)], axis=0)
+            )
+        return parts
+
+    couplings, bases = [], []
+    for p, q in zip(packed[::2], packed[1::2]):
+        couplings.append(
+            jnp.concatenate([jnp.where(lane32, p, swap(q)), jnp.where(lane32, swap(p), q)], axis=0)
+        )
+    for c in couplings:
+        parts = split(c)
+        bases.append(dot3(parts, tuple(diagonal(part) for part in parts), NT))
+    t1 = [b - 0.5 * unit for b in bases]
+    d1 = [pairs(t) for t in t1]
+    t2 = [times(t, d) for t, d in zip(t1, d1)]
+    t3 = [times(t, d) for t, d in zip(t2, d1)]
+    t4 = [once(t, diagonal(t.astype(BF))) for t in t2]
+    d4 = [diagonal(t.astype(BF)) for t in t4]
+
+    def cubic(i, k):
+        return SERIES[k] * unit + SERIES[k + 1] * t1[i] + (SERIES[k + 2] * t2[i] + SERIES[k + 3] * t3[i])
+
+    g = [cubic(i, 8) + SERIES[12] * t4[i] for i in range(count)]
+    g = [cubic(i, 4) + once(v, d) for i, (v, d) in enumerate(zip(g, d4))]
+    g = [cubic(i, 0) + once(v, d) for i, (v, d) in enumerate(zip(g, d4))]
+    turned = [swap(c) for c in couplings]
+    upright = [jnp.concatenate([c, s], axis=0).T[0:64] for c, s in zip(couplings, turned)]
+    out = []
+    for i in range(count):
+        b, c, s = bases[i], couplings[i], turned[i]
+        y = dot3(split(g[i]), beside(jnp.where(left, b, s), jnp.where(left, swap(b), c)))
+        tops = [y[:, 0:128] + jnp.where(lane == row, ORIGIN, 0.0), y[:, 128:256] + jnp.where(lane == row, ORIGIN, 0.0)]
+        y = dot3(split(jnp.concatenate([upright[i], b], axis=0)), beside(*tops))
+        for h in range(2):
+            z = y[:, 128 * h : 128 * h + 128]
+            top = jnp.where(left, tops[h], -(ORIGIN * (s, c)[h] + z[64:128]))
+            bottom = z[0:64] + jnp.where(right_unit, ORIGIN, 0.0)
+            out.append(jnp.concatenate([top, bottom], axis=0))
+    return out
 
 
 def tree(pieces):
@@ -39,7 +144,7 @@
 
 def kernel(
     order_ref, xt_ref, out_ref,
-    first0, first1, second0, second1, export, arrive, outbox, inbox, part, gather1, gather2, total, turn, final,
+    first0, first1, second0, second1, export, arrive, outbox, inbox, part, gather1, gather2, total, leave, turn, final,
     send1, recv1, send2, recv2, send3, recv3, sendx, recvx, sendb, recvb, sendf, recvf,
 ):
     row = lax.axis_index("row")
@@ -50,14 +155,14 @@
     side = (y_low + y_high) % 2
     sibling = pair + 1 - 2 * core
     firsts, seconds = (first0, first1), (second0, second1)
-    me1 = x * 2 + side
-    me2 = z * 2 + y_high
-
-    def sharer(j):
-        return (z * 2 + (j + y_high) % 2, ((j // 2) * 2 + y_high) * 2 + core)
-
-    def holder(j):
-        return ((j // 2) * 2 + (side + j) % 2, (x * 2 + j % 2) * 2 + core)
+    along_x, along_z = [], []
+    for d, e in ((2, 1), (1, 1), (3, 1), (2, 0), (0, 1), (1, 0), (3, 0)):
+        u, v = (x + d) % 4, (side + e) % 2
+        along_x.append((u * 2 + v, z * 2 + (v + y_high) % 2, u * 2 + y_high))
+        u, v = (z + d) % 4, (y_high + e) % 2
+        along_z.append((u * 2 + v, u * 2 + (side + v) % 2, x * 2 + v))
+    sharers, holders = (along_x, along_z), (along_z, along_x)
+    mine, held = (x * 2 + side, z * 2 + y_high), (z * 2 + y_high, x * 2 + side)
 
     lanes = xt_ref.shape[2]
     here = pl.ds(pl.multiple_of(core * lanes, lanes), lanes)
@@ -68,9 +173,9 @@
     def greet(device):
         pl.semaphore_signal(barrier, inc=1, device_id=device, device_id_type=MESH)
 
-    for d in range(1, 8):
-        greet(sharer((me1 + d) % 8))
-        greet(holder((me2 + d) % 8))
+    for _, r, c in along_x + along_z:
+        greet((r, 2 * c))
+        greet((r, 2 * c + 1))
     for d in range(1, 2 * CHIPS):
         greet((row, (pair + d) % (2 * CHIPS)))
 
@@ -80,7 +185,7 @@
 
     for b in range(2 * SLOTS):
         outbox[b] = xt_ref[order_ref[position(1 - core, b)]]
-    pl.semaphore_wait(barrier, 14 + 2 * CHIPS - 1)
+    pl.semaphore_wait(barrier, 28 + 2 * CHIPS - 1)
     swap = pltpu.make_async_remote_copy(
         src_ref=outbox, dst_ref=inbox, send_sem=sendb, recv_sem=recvb,
         device_id=(row, sibling), device_id_type=MESH,
@@ -99,14 +204,7 @@
         state[b % SLOTS, WIDTH:, there] = low
 
     lane32 = lax.broadcasted_iota(jnp.int32, (32, 128), 1)
-    lane64 = lax.broadcasted_iota(jnp.int32, (64, 128), 1)
-    sub64 = lax.broadcasted_iota(jnp.int32, (64, 128), 0)
-    unit = (
-        lax.broadcasted_iota(jnp.int32, (128, 128), 0)
-        == lax.broadcasted_iota(jnp.int32, (128, 128), 1)
-    ).astype(F32)
     ones = jnp.ones((8, 256), BF)
-    minus_sign = (2 * core - 1).astype(F32)
 
     def bulk(buffer, sem):
         return pltpu.make_async_copy(buffer, buffer, sem)
@@ -126,75 +224,65 @@
         squares = jnp.concatenate(split(jnp.concatenate(squares, axis=0)), axis=1)
         part[now, j, 32:40] = lax.dot_general(ones, squares, NT, preferred_element_type=F32)
 
+    def send(source, target, sends, arrivals, device):
+        pltpu.make_async_remote_copy(
+            src_ref=source, dst_ref=target, send_sem=sends, recv_sem=arrivals,
+            device_id=device, device_id_type=MESH,
+        ).start()
+
     def send_parts(now):
-        for d in range(1, 8):
-            j = (me1 + d) % 8
-            pltpu.make_async_remote_copy(
-                src_ref=part.at[now, j], dst_ref=gather1.at[now, me1],
-                send_sem=send1.at[now], recv_sem=recv1.at[now],
-                device_id=sharer(j), device_id_type=MESH,
-            ).start()
-        gather1[now, me1] = part[now, me1]
+        for k in range(2):
+
+            @pl.when(core == k)
+            def _():
+                for j, r, c in sharers[k]:
+                    send(part.at[now, j], gather1.at[now, k, mine[k]], send1.at[now], recv1.at[now, k], (r, 2 * c + 1))
+                if k:
+                    gather1[now, k, mine[k]] = part[now, mine[k]]
+                else:
+                    send(
+                        part.at[now, mine[k]], gather1.at[now, k, mine[k]], send1.at[now], recv1.at[now, k],
+                        (row, sibling),
+                    )
 
     def rotations(now):
-        bulk(gather1.at[now, pl.ds(0, 7)], recv1.at[now]).wait()
-        gather2[now, me2] = tree([gather1[now, s] for s in range(8)])
-        for d in range(1, 8):
-            pltpu.make_async_remote_copy(
-                src_ref=gather2.at[now, me2], dst_ref=gather2.at[now, me2],
-                send_sem=send2.at[now], recv_sem=recv2.at[now],
-                device_id=holder((me2 + d) % 8), device_id_type=MESH,
-            ).start()
-        bulk(gather2.at[now, pl.ds(0, 7)], recv2.at[now]).wait()
-        total[now, me1] = tree([gather2[now, s] for s in range(8)])
-        for d in range(1, 8):
-            pltpu.make_async_remote_copy(
-                src_ref=total.at[now, me1], dst_ref=total.at[now, me1],
-                send_sem=send3.at[now], recv_sem=recv3.at[now],
-                device_id=sharer((me1 + d) % 8), device_id_type=MESH,
-            ).start()
-        bulk(total.at[now, pl.ds(0, 7)], recv3.at[now]).wait()
-        bulk(part.at[now, pl.ds(0, 7)], send1.at[now]).wait()
-        bulk(gather2.at[now, pl.ds(0, 7)], send2.at[now]).wait()
-        bulk(total.at[now, pl.ds(0, 7)], send3.at[now]).wait()
-
-        skews = []
+        @pl.when(core == 1)
+        def _():
+            for k in (1, 0):
+                bulk(gather1.at[now, k, pl.ds(0, 8 - k)], recv1.at[now, k]).wait()
+                gather2[now, k, held[k]] = tree([gather1[now, k, s] for s in range(8)])
+                for _, r, c in holders[k]:
+                    place = gather2.at[now, k, held[k]]
+                    send(place, place, send2.at[now], recv2.at[now, k], (r, 2 * c + 1))
+            for k in (1, 0):
+                bulk(gather2.at[now, k, pl.ds(0, 7)], recv2.at[now, k]).wait()
+                found = coupling(tree([gather2[now, k, s] for s in range(8)]), 1.0 - 2.0 * k)
+                place = total.at[now, mine[k]]
+                if k:
+                    total[now, mine[k]] = found
+                    source = place
+                else:
+                    leave[now] = found
+                    source = leave.at[now]
+                for _, r, c in sharers[k]:
+                    send(source, place, send3.at[now], recv3.at[now], (r, 2 * c + k))
+                if not k:
+                    send(source, place, send3.at[now], recv3.at[now], (row, sibling))
+            bulk(total.at[now, pl.ds(0, 7)], recv3.at[now]).wait()
+            bulk(part.at[now, pl.ds(0, 7)], send1.at[now]).wait()
+            for k in range(2):
+                bulk(gather2.at[now, k, pl.ds(0, 7)], send2.at[now]).wait()
+            bulk(total.at[now], send3.at[now]).wait()
+            bulk(total.at[now, pl.ds(0, 7)], send3.at[now]).wait()
+
+        @pl.when(core == 0)
+        def _():
+            bulk(total.at[now], recv3.at[now]).wait()
+            bulk(part.at[now], send1.at[now]).wait()
+
+        turns = turn_matrices([total[now, j] for j in range(SLOTS)])
         for j in range(SLOTS):
-            packed = total[now, j, 0:32]
-            inverse = lax.rsqrt(total[now, j, 32:40] + 1e-06)[0:1]
-            turned = pltpu.roll(packed, 64, 1)
-            cross = jnp.concatenate(
-                [jnp.where(lane32 < 64, packed, turned), jnp.where(lane32 < 64, turned, packed)], axis=0
-            )
-            column = jnp.sum(jnp.where(lane64 == sub64, inverse, 0.0), axis=1, keepdims=True)
-            cosine = jnp.where(lane64 >= 64, cross * inverse, 0.0) * column
-            frobenius = jnp.sqrt(jnp.sum(cosine * cosine, axis=(0, 1), keepdims=True))
-            upper = jnp.concatenate([cosine * (minus_sign / (1.0 + frobenius)), jnp.zeros((64, 128), F32)], axis=0)
-            skews.append(upper - upper.T)
-        e0, w0, e1, w1, e2 = [], [], [], [], []
-        for k in skews:
-            high, low = split(k)
-            m = lax.dot_general(
-                jnp.concatenate([high, low], axis=1),
-                jnp.concatenate(
-                    [jnp.concatenate([high, high], axis=1), jnp.concatenate([low, low], axis=1)], axis=0
-                ),
-                NT, preferred_element_type=F32,
-            )
-            e0.append(0.5 * (unit - (m[:, 0:128] + m[:, 128:256])))
-        for j in range(SLOTS):
-            parts = split(e0[j])
-            e1.append((product(parts, parts), 0.75 * unit + 0.25 * e0[j]))
-            w0.append(product(split(unit + skews[j]), split(unit + 0.5 * e0[j])))
-        e1 = [product(split(a), split(b)) for a, b in e1]
-        for j in range(SLOTS):
-            parts = split(e1[j])
-            e2.append((product(parts, parts), 0.75 * unit + 0.25 * e1[j]))
-            w1.append(product(split(w0[j]), split(unit + 0.5 * e1[j])))
-        e2 = [product(split(a), split(b)) for a, b in e2]
-        for j in range(SLOTS):
-            r = product(split(w1[j]), split(unit + 0.5 * e2[j])) * (1.0 / math.sqrt(2.0))
-            high, low = split(r)
+            high, low = split(turns[j])
             turn[j, :, 0:128] = high
             turn[j, :, 128:256] = low
             turn[j, :, 256:384] = high
@@ -325,12 +413,13 @@
             pltpu.VMEM((2 * SLOTS, WIDTH, rows), F32),
             pltpu.VMEM((2 * SLOTS, WIDTH, rows), F32),
             pltpu.VMEM((2, SLOTS, PART, 128), F32),
-            pltpu.VMEM((2, 8, PART, 128), F32),
-            pltpu.VMEM((2, 8, PART, 128), F32),
-            pltpu.VMEM((2, SLOTS, PART, 128), F32),
+            pltpu.VMEM((2, 2, 8, PART, 128), F32),
+            pltpu.VMEM((2, 2, 8, PART, 128), F32),
+            pltpu.VMEM((2, SLOTS, 32, 128), F32),
+            pltpu.VMEM((2, 32, 128), F32),
             pltpu.VMEM((SLOTS, 128, 384), BF),
             pltpu.VMEM((2 * SLOTS, WIDTH, wide), F32),
-            dma((2,)), dma((2,)), dma((2,)), dma((2,)), dma((2,)), dma((2,)), dma((2,)), dma((2,)),
+            dma((2,)), dma((2, 2)), dma((2,)), dma((2, 2)), dma((2,)), dma((2,)), dma((2,)), dma((2,)),
             dma(()), dma(()), dma((2 * SLOTS,)), dma((CHIPS, 2)),
         ],
         compiler_params=pltpu.CompilerParams(

time: 267 us -> 224 us (0.84)
  Pallas kernels: 257 us -> 214 us
    pallas_call x1, Pallas kernels: 257 us -> 214 us  [per_device(): pl.pallas_call(kernel, out_shape=jax.ShapeDtypeStruct((CHIPS, 2 * WIDTH,...]
where the time goes in v2:
time: 224 us; the launch traced here: 220 us
  Pallas kernels  214 us (96%)
  local copies, waits for them, and re-layouts  6.3 us (3%)
    pallas_call x1, Pallas kernels, per_device(): pl.pallas_call(kernel, out_shape=jax.ShapeDtypeStruct((CHIPS, 2 * WIDTH,...  214 us

profile of v2, /device:TPU:1, one launch (start us, length us, event | category | flops | bytes accessed | tf_op | source)
XLA Modules:
  0.0 220.3 jit_solution(12764135637541645861)
XLA Ops:
  0.0 0.0 copy-start.1
  0.0 2.9 %copy.4 = f32[2048,256]{1,0:T(8,128)} copy(f32[2048,256]{0,1:T(8,128)} %bitcast.6) | data formatting | bytes 4194304 | tf_op jit(solution)/shard_map/transpose | solution.py:399
  2.9 0.0 copy-done.1
  2.9 0.0 copy-start
  2.9 1.6 copy-done
  4.5 214.0 %shard_map.28 = f32[8,128,512]{2,1,0:T(8,128)S(1)} custom-call(s32[32]{0:T(128)S(1)} %copy-done.1, f32[32,64,256]{2,1,0:T(8,128)S(1)} %bitcast.5), custom_call_target="tpu_custom_call" | custom-call | tf_op jit(solution)/shard_map/pallas_call | solution.py:401
  218.5 1.8 copy.5
Async XLA Ops:
  0.0 2.9 %copy-start.1 = (s32[32]{0:T(128)S(1)}, s32[32]{0:T(128)}, u32[]{:S(2)}) copy-start(s32[32]{0:T(128)} %order_ref.1) | copy-start | bytes 388
  2.9 1.6 copy-start

commit v3 on v2

--- a/solution.py
+++ b/solution.py
@@ -12,7 +12,7 @@
 CHIPS = 8
 SLOTS = 8
 WIDTH = 64
-PART = 40
+PART = 33
 MESH = pl.DeviceIdType.MESH
 BF = jnp.bfloat16
 F32 = jnp.float32
@@ -49,7 +49,7 @@
     lane = lax.broadcasted_iota(jnp.int32, (32, 128), 1)
     row = lax.broadcasted_iota(jnp.int32, (32, 128), 0)
     left = lane < 64
-    inverse = lax.rsqrt(sums[32:40] + 1e-06)
+    inverse = lax.rsqrt(jnp.broadcast_to(sums[32:33], (8, 128)) + 1e-06)
     across = jnp.where(left[0:1], pltpu.roll(inverse, 64, 1)[0:1], inverse[0:1])
     down = jnp.where(
         left,
@@ -143,9 +143,9 @@
 
 
 def kernel(
-    order_ref, xt_ref, out_ref,
-    first0, first1, second0, second1, export, arrive, outbox, inbox, part, gather1, gather2, total, leave, turn, final,
-    send1, recv1, send2, recv2, send3, recv3, sendx, recvx, sendb, recvb, sendf, recvf,
+    order_ref, x_ref, out_ref,
+    loaded, xt_ref, first0, first1, second0, second1, export, arrive, outbox, inbox, part, gather1, gather2, total, leave, turn, final,
+    send1, recv1, send2, recv2, send3, recv3, sendx, recvx, sendb, recvb, sendf, recvf, loads,
 ):
     row = lax.axis_index("row")
     pair = lax.axis_index("pair")
@@ -168,6 +168,11 @@
     here = pl.ds(pl.multiple_of(core * lanes, lanes), lanes)
     there = pl.ds(pl.multiple_of((1 - core) * lanes, lanes), lanes)
 
+    chunk = loaded.shape[1] // 4
+    columns = [pl.ds(chunk * q, chunk) for q in range(4)]
+    copies = [pltpu.make_async_copy(x_ref.at[:, c], loaded.at[:, c], loads.at[q]) for q, c in enumerate(columns)]
+    for copy in copies:
+        copy.start()
     barrier = pltpu.get_barrier_semaphore()
 
     def greet(device):
@@ -178,6 +183,13 @@
         greet((r, 2 * c + 1))
     for d in range(1, 2 * CHIPS):
         greet((row, (pair + d) % (2 * CHIPS)))
+
+    for q, copy in enumerate(copies):
+        copy.wait()
+        for u in range(chunk // 128 * q, chunk // 128 * (q + 1)):
+            tile = loaded[:, 128 * u : 128 * u + 128].T
+            xt_ref[2 * u] = tile[0:WIDTH]
+            xt_ref[2 * u + 1] = tile[WIDTH:]
 
     def position(owner, block):
         plain = 2 * (block % SLOTS) + block // SLOTS
@@ -222,7 +234,7 @@
             u = u * u
             squares.append(u[:, 0:128] + u[:, 128:256] + (u[:, 256:384] + u[:, 384:512]))
         squares = jnp.concatenate(split(jnp.concatenate(squares, axis=0)), axis=1)
-        part[now, j, 32:40] = lax.dot_general(ones, squares, NT, preferred_element_type=F32)
+        part[now, j, 32:33] = lax.dot_general(ones, squares, NT, preferred_element_type=F32)[0:1]
 
     def send(source, target, sends, arrivals, device):
         pltpu.make_async_remote_copy(
@@ -332,7 +344,7 @@
             final[2 - 2 * core if j == 0 else 2 * j - 1] = b
 
         def place(d):
-            m = ((chip % 4) * 4 + d) % 16
+            m = ((chip + d) % 4) * 4 + d // 4
             n = m + m // 15
             n = n + core * (31 - 2 * n)
             return m, n // 2, n % 2
@@ -396,14 +408,15 @@
 def per_device(snapshots, start_order):
     rows = snapshots.shape[0]
     wide = 2 * rows
-    transposed = snapshots.T.reshape(4 * SLOTS, WIDTH, rows)
     dma = pltpu.SemaphoreType.DMA
     blocks = pl.pallas_call(
         kernel,
         out_shape=jax.ShapeDtypeStruct((CHIPS, 2 * WIDTH, wide), F32),
-        in_specs=[pl.BlockSpec(memory_space=pltpu.SMEM), pl.BlockSpec(memory_space=pltpu.VMEM)],
+        in_specs=[pl.BlockSpec(memory_space=pltpu.SMEM), pl.BlockSpec(memory_space=pl.ANY)],
         out_specs=pl.BlockSpec(memory_space=pl.ANY),
         scratch_shapes=[
+            pltpu.VMEM(snapshots.shape, F32),
+            pltpu.VMEM((4 * SLOTS, WIDTH, rows), F32),
             pltpu.VMEM((SLOTS, 2 * WIDTH, wide), BF),
             pltpu.VMEM((SLOTS, 2 * WIDTH, wide), BF),
             pltpu.VMEM((SLOTS, 2 * WIDTH, wide), BF),
@@ -420,12 +433,12 @@
             pltpu.VMEM((SLOTS, 128, 384), BF),
             pltpu.VMEM((2 * SLOTS, WIDTH, wide), F32),
             dma((2,)), dma((2, 2)), dma((2,)), dma((2, 2)), dma((2,)), dma((2,)), dma((2,)), dma((2,)),
-            dma(()), dma(()), dma((2 * SLOTS,)), dma((CHIPS, 2)),
+            dma(()), dma(()), dma((2 * SLOTS,)), dma((CHIPS, 2)), dma((4,)),
         ],
         compiler_params=pltpu.CompilerParams(
             collective_id=0, has_side_effects=True, vmem_limit_bytes=40 * 1024 * 1024
         ),
-    )(start_order, transposed)
+    )(start_order, snapshots)
     return blocks.transpose(0, 2, 1).reshape(CHIPS * wide, 2 * WIDTH)
 
 

time: 224 us -> 216 us (0.964); the launches traced: 220 us -> 216 us
  local copies, waits for them, and re-layouts: 6.3 us -> 4.06 us
    transpose x1 -> x0, local copies, waits for them, and re-layouts: 2.89 us -> none  [per_device(): transposed = snapshots.T.reshape(4 * SLOTS, WIDTH, rows)]
    pallas_call x1, Pallas kernels: 214 us -> 212 us  [per_device(): pl.pallas_call(kernel, out_shape=jax.ShapeDtypeStruct((CHIPS, 2 * WIDTH,...]
where the time goes in v3:
time: 216 us
  Pallas kernels  212 us (98%)
  local copies, waits for them, and re-layouts  4.06 us (2%)
    pallas_call x1, Pallas kernels, per_device(): pl.pallas_call(kernel, out_shape=jax.ShapeDtypeStruct((CHIPS, 2 * WIDTH,...  212 us

profile of v3, /device:TPU:1, one launch (start us, length us, event | category | flops | bytes accessed | tf_op | source)
XLA Modules:
  0.0 215.6 jit_solution(9611997761348231508)
XLA Ops:
  0.0 0.0 copy-start
  0.0 1.6 copy-done
  1.6 0.0 copy-start.1
  1.6 0.7 copy-done.1
  2.2 211.5 %shard_map.28 = f32[8,128,512]{2,1,0:T(8,128)S(1)} custom-call(s32[32]{0:T(128)S(1)} %copy-done.1, f32[256,2048]{1,0:T(8,128)S(1)} %copy-done), custom_call_target="tpu_custom_call" | custom-call | tf_op jit(solution)/shard_map/pallas_call | solution.py:412
  213.8 1.8 copy.3
Async XLA Ops:
  0.0 1.6 copy-start
  1.6 0.7 copy-start.1

commit v4 on v3

--- a/solution.py
+++ b/solution.py
@@ -122,18 +122,21 @@
     g = [cubic(i, 0) + once(v, d) for i, (v, d) in enumerate(zip(g, d4))]
     turned = [swap(c) for c in couplings]
     upright = [jnp.concatenate([c, s], axis=0).T[0:64] for c, s in zip(couplings, turned)]
-    out = []
-    for i in range(count):
+
+    def pair_of(i):
         b, c, s = bases[i], couplings[i], turned[i]
         y = dot3(split(g[i]), beside(jnp.where(left, b, s), jnp.where(left, swap(b), c)))
         tops = [y[:, 0:128] + jnp.where(lane == row, ORIGIN, 0.0), y[:, 128:256] + jnp.where(lane == row, ORIGIN, 0.0)]
         y = dot3(split(jnp.concatenate([upright[i], b], axis=0)), beside(*tops))
+        out = []
         for h in range(2):
             z = y[:, 128 * h : 128 * h + 128]
             top = jnp.where(left, tops[h], -(ORIGIN * (s, c)[h] + z[64:128]))
             bottom = z[0:64] + jnp.where(right_unit, ORIGIN, 0.0)
             out.append(jnp.concatenate([top, bottom], axis=0))
-    return out
+        return out
+
+    return pair_of
 
 
 def tree(pieces):
@@ -216,25 +219,28 @@
         state[b % SLOTS, WIDTH:, there] = low
 
     lane32 = lax.broadcasted_iota(jnp.int32, (32, 128), 1)
-    ones = jnp.ones((8, 256), BF)
+    lane8 = lax.broadcasted_iota(jnp.int32, (8, 128), 1) < 64
 
     def bulk(buffer, sem):
         return pltpu.make_async_copy(buffer, buffer, sem)
 
-    def crossing(now, j):
+    def sums_of_squares(u):
+        u = u * u
+        u = u[:, 0:128] + u[:, 128:256] + (u[:, 256:384] + u[:, 384:512])
+        return jnp.broadcast_to(jnp.sum(u.T, axis=0, keepdims=True), (8, 128))
+
+    def crossing(now, j, norms=None):
         a = firsts[now][j]
         b = seconds[now][j]
         grown = lax.dot_general(a, b, NT, preferred_element_type=F32)
         grown = grown[0:64] + grown[64:128]
         both = grown + pltpu.roll(grown, 64, 1)
         part[now, j, 0:32] = jnp.where(lane32 < 64, both[0:32], both[32:64])
-        squares = []
-        for v in (a, b):
-            u = v[0:64].astype(F32) + v[64:128].astype(F32)
-            u = u * u
-            squares.append(u[:, 0:128] + u[:, 128:256] + (u[:, 256:384] + u[:, 384:512]))
-        squares = jnp.concatenate(split(jnp.concatenate(squares, axis=0)), axis=1)
-        part[now, j, 32:33] = lax.dot_general(ones, squares, NT, preferred_element_type=F32)[0:1]
+        if norms is None:
+            norms = sums_of_squares(
+                jnp.concatenate([v[0:64].astype(F32) + v[64:128].astype(F32) for v in (a, b)], axis=0)
+            )
+        part[now, j, 32:33] = norms[0:1]
 
     def send(source, target, sends, arrivals, device):
         pltpu.make_async_remote_copy(
@@ -292,9 +298,11 @@
             bulk(total.at[now], recv3.at[now]).wait()
             bulk(part.at[now], send1.at[now]).wait()
 
-        turns = turn_matrices([total[now, j] for j in range(SLOTS)])
-        for j in range(SLOTS):
-            high, low = split(turns[j])
+        return turn_matrices([total[now, j] for j in range(SLOTS)])
+
+    def keep(pair_of, i):
+        for j, r in zip((2 * i, 2 * i + 1), pair_of(i)):
+            high, low = split(r)
             turn[j, :, 0:128] = high
             turn[j, :, 128:256] = low
             turn[j, :, 256:384] = high
@@ -304,17 +312,19 @@
         high = jnp.concatenate([a[j, 0:WIDTH], b[j, 0:WIDTH]], axis=0)
         low = jnp.concatenate([a[j, WIDTH:], b[j, WIDTH:]], axis=0)
         r = jnp.dot(turn[j], jnp.concatenate([high, high, low], axis=0), preferred_element_type=F32)
-        return r[0:WIDTH], r[WIDTH:]
+        return r[0:WIDTH], r[WIDTH:], sums_of_squares(r)
 
     def put(state, j, v):
         high, low = split(v)
         state[j, 0:WIDTH] = high
         state[j, WIDTH:] = low
 
-    def advance(now):
+    def advance(now, pair_of):
         later = 1 - now
         first, second = firsts[later], seconds[later]
-        a, b = apply(now, SLOTS - 1)
+        keep(pair_of, SLOTS // 2 - 1)
+        norms = [None] * SLOTS
+        a, b, norms[7] = apply(now, SLOTS - 1)
         export[now] = a
         swap = pltpu.make_async_remote_copy(
             src_ref=export.at[now], dst_ref=arrive.at[now],
@@ -323,23 +333,30 @@
         )
         swap.start()
         put(second, SLOTS - 2, b)
-        a, b = apply(now, 0)
+        for i in range(SLOTS // 2 - 1):
+            keep(pair_of, i)
+        a, b, norms[0] = apply(now, 0)
         put(first, core, a)
         put(first, 1 - core, b)
         for j in range(1, SLOTS - 1):
-            a, b = apply(now, j)
+            a, b, norms[j] = apply(now, j)
             put(first, j + 1, a)
             put(second, j - 1, b)
+        halves = norms[0], pltpu.roll(norms[0], 64, 1)
+        lead = [jnp.where(core == 0, *halves), jnp.where(core == 0, halves[1], halves[0])] + norms[1 : SLOTS - 1]
         for j in range(SLOTS - 1):
-            crossing(later, j)
+            crossing(later, j, jnp.where(lane8, lead[j], norms[j + 1]))
         swap.wait()
-        put(second, SLOTS - 1, arrive[now])
-        crossing(later, SLOTS - 1)
+        came = arrive[now]
+        put(second, SLOTS - 1, came)
+        crossing(later, SLOTS - 1, jnp.where(lane8, lead[SLOTS - 1], sums_of_squares(jnp.concatenate([came, came], axis=0))))
         send_parts(later)
 
-    def finish():
+    def finish(pair_of):
+        for i in range(SLOTS // 2):
+            keep(pair_of, i)
         for j in range(SLOTS):
-            a, b = apply(1, j)
+            a, b, _ = apply(1, j)
             final[2 * core if j == 0 else min(2 * j + 2, 15)] = a
             final[2 - 2 * core if j == 0 else 2 * j - 1] = b
 
@@ -388,17 +405,16 @@
     send_parts(0)
 
     def two_steps(i, carry):
-        rotations(0)
-        advance(0)
-        rotations(1)
+        advance(0, rotations(0))
+        pair_of = rotations(1)
 
         @pl.when(i < STEPS // 2 - 1)
         def _():
-            advance(1)
+            advance(1, pair_of)
 
         @pl.when(i == STEPS // 2 - 1)
         def _():
-            finish()
+            finish(pair_of)
 
         return carry
 

time: 216 us -> 215 us (level)
  no operation moved by 1% of the time
where the time goes in v4:
time: 215 us; the launch traced here: 214 us
  Pallas kernels  210 us (98%)
  local copies, waits for them, and re-layouts  4.06 us (2%)
    pallas_call x1, Pallas kernels, per_device(): pl.pallas_call(kernel, out_shape=jax.ShapeDtypeStruct((CHIPS, 2 * WIDTH,...  210 us

profile of v4, /device:TPU:1, one launch (start us, length us, event | category | flops | bytes accessed | tf_op | source)
XLA Modules:
  0.0 214.4 jit_solution(12189534813807371717)
XLA Ops:
  0.0 0.0 copy-start
  0.0 1.6 copy-done
  1.6 0.0 copy-start.1
  1.6 0.7 copy-done.1
  2.2 210.4 %shard_map.28 = f32[8,128,512]{2,1,0:T(8,128)S(1)} custom-call(s32[32]{0:T(128)S(1)} %copy-done.1, f32[256,2048]{1,0:T(8,128)S(1)} %copy-done), custom_call_target="tpu_custom_call" | custom-call | tf_op jit(solution)/shard_map/pallas_call | solution.py:428
  212.6 1.8 copy.3
Async XLA Ops:
  0.0 1.6 copy-start
  1.6 0.7 copy-start.1

commit v5 on v4

--- a/solution.py
+++ b/solution.py
@@ -57,7 +57,8 @@
         jnp.sum(jnp.where(lane == row + 32, inverse[0:1], 0.0), axis=1, keepdims=True),
     )
     cosine = sums[0:32] * across * down
-    frobenius = jnp.sqrt(jnp.sum(cosine * cosine, axis=(0, 1), keepdims=True))
+    squares = jnp.sum(tree([cosine[i : i + 8] * cosine[i : i + 8] for i in range(0, 32, 8)]), axis=0, keepdims=True)
+    frobenius = jnp.sqrt(jnp.sum(squares, axis=1, keepdims=True))
     return cosine * (sign / (1.0 + frobenius))
 
 
@@ -107,33 +108,41 @@
     for c in couplings:
         parts = split(c)
         bases.append(dot3(parts, tuple(diagonal(part) for part in parts), NT))
+    turned = [swap(c) for c in couplings]
+    uprights = [jnp.concatenate([c, s], axis=0).T[0:64] for c, s in zip(couplings, turned)]
     t1 = [b - 0.5 * unit for b in bases]
-    d1 = [pairs(t) for t in t1]
-    t2 = [times(t, d) for t, d in zip(t1, d1)]
-    t3 = [times(t, d) for t, d in zip(t2, d1)]
-    t4 = [once(t, diagonal(t.astype(BF))) for t in t2]
-    d4 = [diagonal(t.astype(BF)) for t in t4]
+    y0 = [jnp.concatenate([u, b], axis=0) for u, b in zip(uprights, bases)]
+    both = [times(jnp.concatenate([t, y], axis=0), pairs(t)) for t, y in zip(t1, y0)]
+    t2, y1 = [v[0:64] for v in both], [v[64:192] for v in both]
+    both = [times(jnp.concatenate([t, a, b], axis=0), pairs(t)) for t, a, b in zip(t2, y0, y1)]
+    d4 = [diagonal(v[0:64].astype(BF)) for v in both]
+    y2, y3 = [v[64:192] for v in both], [v[192:320] for v in both]
 
     def cubic(i, k):
-        return SERIES[k] * unit + SERIES[k + 1] * t1[i] + (SERIES[k + 2] * t2[i] + SERIES[k + 3] * t3[i])
-
-    g = [cubic(i, 8) + SERIES[12] * t4[i] for i in range(count)]
+        return SERIES[k] * y0[i] + SERIES[k + 1] * y1[i] + (SERIES[k + 2] * y2[i] + SERIES[k + 3] * y3[i])
+
+    y4 = [once(y, d) for y, d in zip(y0, d4)]
+    g = [cubic(i, 8) + SERIES[12] * y4[i] for i in range(count)]
     g = [cubic(i, 4) + once(v, d) for i, (v, d) in enumerate(zip(g, d4))]
     g = [cubic(i, 0) + once(v, d) for i, (v, d) in enumerate(zip(g, d4))]
-    turned = [swap(c) for c in couplings]
-    upright = [jnp.concatenate([c, s], axis=0).T[0:64] for c, s in zip(couplings, turned)]
+    at_left = jnp.where(lane == row, 1.0, 0.0)
+    tops = [beside(jnp.where(left, at_left, s), jnp.where(left, at_left, c)) for c, s in zip(couplings, turned)]
+    bottoms = [
+        beside(jnp.where(left, b, s), jnp.where(left, swap(b), c)) for b, c, s in zip(bases, couplings, turned)
+    ]
 
     def pair_of(i):
-        b, c, s = bases[i], couplings[i], turned[i]
-        y = dot3(split(g[i]), beside(jnp.where(left, b, s), jnp.where(left, swap(b), c)))
-        tops = [y[:, 0:128] + jnp.where(lane == row, ORIGIN, 0.0), y[:, 128:256] + jnp.where(lane == row, ORIGIN, 0.0)]
-        y = dot3(split(jnp.concatenate([upright[i], b], axis=0)), beside(*tops))
+        up = dot3(split(ORIGIN * unit + g[i][64:128]), tops[i])
+        down = dot3(split(g[i][0:64]), bottoms[i])
         out = []
-        for h in range(2):
-            z = y[:, 128 * h : 128 * h + 128]
-            top = jnp.where(left, tops[h], -(ORIGIN * (s, c)[h] + z[64:128]))
-            bottom = z[0:64] + jnp.where(right_unit, ORIGIN, 0.0)
-            out.append(jnp.concatenate([top, bottom], axis=0))
+        for h, tall in enumerate((uprights[i], swap(uprights[i]))):
+            place = slice(128 * h, 128 * h + 128)
+            top = jnp.where(left, up[:, place], -up[:, place])
+            out.append(
+                jnp.concatenate(
+                    [top, down[:, place] + ORIGIN * jnp.where(left, tall, jnp.where(right_unit, 1.0, 0.0))], axis=0
+                )
+            )
         return out
 
     return pair_of

time: 215 us -> 214 us (level)
  no operation moved by 1% of the time
where the time goes in v5:
time: 214 us
  Pallas kernels  210 us (98%)
  local copies, waits for them, and re-layouts  4.06 us (2%)
    pallas_call x1, Pallas kernels, per_device(): pl.pallas_call(kernel, out_shape=jax.ShapeDtypeStruct((CHIPS, 2 * WIDTH,...  210 us

profile of v5, /device:TPU:1, one launch (start us, length us, event | category | flops | bytes accessed | tf_op | source)
XLA Modules:
  0.0 213.7 jit_solution(17925572364021070155)
XLA Ops:
  0.0 0.0 copy-start
  0.0 1.6 copy-done
  1.6 0.0 copy-start.1
  1.6 0.7 copy-done.1
  2.2 209.6 %shard_map.28 = f32[8,128,512]{2,1,0:T(8,128)S(1)} custom-call(s32[32]{0:T(128)S(1)} %copy-done.1, f32[256,2048]{1,0:T(8,128)S(1)} %copy-done), custom_call_target="tpu_custom_call" | custom-call | tf_op jit(solution)/shard_map/pallas_call | solution.py:437
  211.9 1.8 copy.3
Async XLA Ops:
  0.0 1.6 copy-start
  1.6 0.7 copy-start.1
